TPU v7x, 32 devices: a whole 2x2x4 slice. The times are simulated.
32 devices in a mesh: batch: 16 (over z, x, core), branch: 2 (over y).
Axes of the slice: x: 2, y: 2, z: 4, core: 2. Of those that a mesh axis runs over, the one named last changes fastest.
Arguments:
- tokens: bfloat16 [25088, 768], P(('batch', 'branch')), may hold values from -6 to 6
- cotangent: bfloat16 [25088, 768], P(('batch', 'branch')), may hold values from -6 to 6
- image_tokens: int32 [16, 8], P('batch'), may hold values from 0 to 784, as said below
- w_qkv: float32 [3, 768, 768], P(None, ('batch', 'branch')), may hold values from -0.21875 to 0.21875
- w_out: float32 [768, 768], P(None, ('batch', 'branch')), may hold values from -0.875 to 0.875
- w_up: float32 [768, 3072], P(('batch', 'branch')), may hold values from -0.21875 to 0.21875
- bias_up: float32 [3072], P(('batch', 'branch')), may hold values from -3 to 3
- w_down: float32 [3072, 768], P(None, ('batch', 'branch')), may hold values from -0.109375 to 0.109375
- bias_down: float32 [768], P(('batch', 'branch')), may hold values from -3 to 3
- norm_gain: float32 [768], P(('batch', 'branch')), may hold values from 0.25 to 1.75
- query_gain: float32 [64], replicated, may hold values from 0.25 to 1.75
- key_gain: float32 [64], replicated, may hold values from 0.25 to 1.75
Outputs:
- block_out: bfloat16 [25088, 768], P(('batch', 'branch'))
- grad_tokens: bfloat16 [25088, 768], P(('batch', 'branch'))
- grad_w_qkv: float32 [3, 768, 768], P(None, ('batch', 'branch'))
- grad_w_out: float32 [768, 768], P(None, ('batch', 'branch'))
- grad_w_up: float32 [768, 3072], P(('batch', 'branch'))
- grad_bias_up: float32 [3072], P(('batch', 'branch'))
- grad_w_down: float32 [3072, 768], P(None, ('batch', 'branch'))
- grad_bias_down: float32 [768], P(('batch', 'branch'))
- grad_norm_gain: float32 [768], P(('batch', 'branch'))
- grad_query_gain: float32 [64], replicated
- grad_key_gain: float32 [64], replicated
Inputs may be any that keep to these rules, and one draw needn't show every extreme that they name: `image_tokens`: row j lists, in order, the token counts of the 8 image slots laid end to end in rows j * 1568 to (j + 1) * 1568 - 1 of tokens; each count is 0, 196 or 784, a row holds at most one count of 784, and each row sums to 1568.
All inputs are finite; a program needn't handle non-finite values.
Results may differ from a plain program's by a relative error of at most 0.02.
Values may be sent and summed in bfloat16 or wider, within the bound.
A program may use at most 320 MiB of HBM per device.

v0:
```python
import functools
import jax
import jax.numpy as jnp
from jax import lax
from jax.experimental import pallas as pl
from jax.experimental.pallas import tpu as pltpu
from jax.sharding import PartitionSpec as P

HD = 64
LANES = 128
NORM_EPS = 1e-06
LONGEST = 784
PATCHES = 196
SLOT = 208
VMEM_CAP = 66_000_000
BF = jnp.bfloat16
F32 = jnp.float32


def dot(a, b, dims=((1,), (0,))):
    return lax.dot_general(a, b, (dims, ((), ())), preferred_element_type=F32)


NT = ((1,), (1,))
TN = ((0,), (0,))


def norm_stats(values):
    centred = values - jnp.mean(values, axis=-1, keepdims=True)
    spread = jnp.mean(centred * centred, axis=-1, keepdims=True)
    scale = lax.rsqrt(spread + NORM_EPS)
    return centred * scale, scale


def head_means(values, ones_low):
    means = []
    for at in range(0, values.shape[1], LANES):
        some = values[:, at : at + LANES]
        high = some.astype(BF)
        low = (some - high.astype(F32)).astype(BF)
        means.append(dot(jnp.concatenate([high, low], axis=1), ones_low))
    return jnp.concatenate(means, axis=1)


def head_ones():
    row = lax.broadcasted_iota(jnp.int32, (2 * LANES, LANES), 0) % LANES // HD
    col = lax.broadcasted_iota(jnp.int32, (2 * LANES, LANES), 1) // HD
    return jnp.where(row == col, 1.0 / HD, 0.0).astype(BF)


def head_stats(raw, ones_low):
    centred = raw - head_means(raw, ones_low)
    scale = lax.rsqrt(head_means(centred * centred, ones_low) + NORM_EPS)
    return centred * scale, scale


MESH = pl.DeviceIdType.MESH


def place():
    return lax.axis_index("batch"), lax.axis_index("branch")


def grid_of(batch):
    chips = batch // 2
    across = 1
    while across * across * 4 <= chips:
        across *= 2
    return chips // across, across


def greet(peers):
    barrier = pltpu.get_barrier_semaphore()
    for peer in peers:
        pl.semaphore_signal(barrier, inc=1, device_id=peer, device_id_type=MESH)
    pl.semaphore_wait(barrier, len(peers))


def neighbours(deep, wide):
    batch, branch = place()
    core, x, z = batch % 2, (batch // 2) % wide, batch // (2 * wide)
    at = lambda zz, xx, cc: (zz * wide + xx) * 2 + cc
    partner = (batch, 1 - branch)
    along_z = [(at((z + s) % deep, x, core), branch) for s in range(1, deep)]
    along_x = [(at(z, (x + s) % wide, core), branch) for s in range(1, wide)]
    sibling = (at(z, x, 1 - core), branch)
    return (z, x, core, branch), partner, along_z, along_x, sibling


def remote(src, dst, send, recv, peer):
    return pltpu.make_async_remote_copy(src_ref=src, dst_ref=dst, send_sem=send, recv_sem=recv, device_id=peer, device_id_type=MESH)


TINY = (8, LANES)
STRIP = 112


def gelu_parts(hidden):
    square = hidden * hidden
    tanh = jnp.tanh(hidden * (0.7978845608028654 + 0.035677408136300125 * square))
    half = 0.5 + 0.5 * tanh
    act = hidden * half
    slope = half + (act * (1.0 - tanh)) * (0.7978845608028654 + 0.1070322244089 * square)
    return act.astype(BF), slope


def repeated(values, count):
    return jnp.concatenate([values] * count, axis=1)


def first_kernel(*refs, deep, wide, cuts, block):
    tokens, cotan, qkv_ref, wo_ref, up_ref, down_ref, nb_ref, db_ref, ub_ref, qg_ref, kg_ref = refs[:11]
    o_x, o_dy, o_normed, o_q, o_k, o_v, o_do, o_qraw, o_kraw, o_heads, o_own, o_other, o_dn = refs[11:24]
    o_sums = (refs[24 : 24 + wide], refs[24 + wide : 24 + 2 * wide])
    gb_ref, gain_ref, bias_ref, tiny = refs[24 + 2 * wide : 28 + 2 * wide]
    scratch = refs[28 + 2 * wide :]
    packs, lands, wires = scratch[:3], scratch[3:6], scratch[6:9]
    rounded, tiny_all, x_par, dy_par, normed, act, d_hid, s_q, s_k, s_v, s_do, s_qraw, s_kraw, s_out, s_dn = scratch[9:24]
    grads, got_core, flats = scratch[24:26], scratch[26:28], scratch[28:31]
    send, recv, tsend, trecv, csend, crecv, osem = scratch[31:]
    (z, x, core, y), partner, along_z, along_x, sibling = neighbours(deep, wide)
    batch = 2 * deep * wide
    own_rows, width = tokens.shape
    shard, hidden = packs[0].shape[1:]
    cols = hidden // 4
    pair = 2 * shard
    direct = pair % 16 == 0
    places = [(b // (2 * wide), (b // 2) % wide, b % 2, s) for b in range(batch) for s in range(2)]

    for half in range(2):
        some = slice(half * cols, (half + 1) * cols)
        packs[0][half] = up_ref[:, half * hidden : (half + 1) * hidden].astype(BF)
        packs[1][half] = down_ref[:, half * hidden : (half + 1) * hidden].astype(BF)
        for at in range(3):
            packs[2][half, :, at * cols : (at + 1) * cols] = qkv_ref[at, :, some].astype(BF)
        packs[2][half, :, 3 * cols :] = wo_ref[...].astype(BF)
    rounded[...] = jnp.zeros(TINY, BF)
    for row, ref in enumerate((nb_ref, db_ref, ub_ref, qg_ref, kg_ref)):
        rounded[row : row + 1, : ref.shape[1]] = ref[...].astype(BF)
    tiny[...] = rounded[...].astype(F32)
    tiny_all[z, x, core, y] = tiny[...]
    greet([partner, sibling] + along_z + along_x)
    outs = []

    def put(src, dst):
        copy = pltpu.make_async_copy(src, dst, osem.at[len(outs)])
        copy.start()
        outs.append(copy)

    spread_tiny = [remote(tiny, tiny_all.at[z, x, core, y], tsend.at[0], trecv.at[0], partner)]
    spread_tiny[0].start()
    over_y = []
    for i, (part, at) in enumerate(cuts):
        over_y.append(remote(packs[part].at[1 - y, :, at], lands[part].at[:, at], send.at[i, 0], recv.at[i, 0], partner))
        over_y[i].start()
    rows_copy = [remote(tokens, x_par, tsend.at[deep + wide], trecv.at[deep + wide], partner), remote(cotan, dy_par, tsend.at[deep + wide + 1], trecv.at[deep + wide + 1], partner)]
    for copy in rows_copy:
        copy.start()

    def tiny_stage(block, peers, first):
        group = [remote(block, block, tsend.at[first + s], trecv.at[first + s], peer) for s, peer in enumerate(peers)]
        for copy in group:
            copy.start()
        for copy in group:
            copy.wait_recv()
        spread_tiny.extend(group)

    over_z, over_x, over_core = [], [], []

    def start_z(i):
        part, at = cuts[i]
        over_y[i].wait_recv()
        mine, other = packs[part][y, :, at].astype(F32), lands[part][:, at].astype(F32)
        pair = jnp.concatenate([jnp.where(y == 0, mine, other), jnp.where(y == 0, other, mine)], axis=0)
        wires[part][z, x, core, :, at] = pair.astype(BF)
        block = wires[part].at[z, x, core, :, at]
        over_z.append([remote(block, block, send.at[i, 1 + s], recv.at[i, 1 + s], peer) for s, peer in enumerate(along_z)])
        for copy in over_z[i]:
            copy.start()

    def start_x(i):
        part, at = cuts[i]
        for copy in over_z[i]:
            copy.wait_recv()
        block = wires[part].at[:, x, core, :, at]
        over_x.append([remote(block, block, send.at[i, deep + s], recv.at[i, deep + s], peer) for s, peer in enumerate(along_x)])
        for copy in over_x[i]:
            copy.start()

    def start_core(i):
        part, at = cuts[i]
        for copy in over_x[i]:
            copy.wait_recv()
        block = wires[part].at[:, :, core, :, at]
        over_core.append(remote(block, block, send.at[i, deep + wide - 1], recv.at[i, deep + wide - 1], sibling))
        over_core[i].start()

    def arrive(i):
        part, at = cuts[i]
        over_core[i].wait_recv()
        if not direct:
            for b in range(batch):
                flats[part][2 * shard * b : 2 * shard * (b + 1), at] = wires[part][b // (2 * wide), (b // 2) % wide, b % 2, :, at]

    def weight(part, at):
        if direct:
            value = wires[part][:, :, :, :, at]
            return value.reshape(width, value.shape[-1])
        return flats[part][:, at]

    for i in range(len(cuts)):
        start_z(i)
        if i == 0:
            spread_tiny[0].wait_recv()
            tiny_stage(tiny_all.at[z, x, core], along_z, 1)
        if i == 1:
            tiny_stage(tiny_all.at[:, x, core], along_x, deep)
        if i == 2:
            tiny_stage(tiny_all.at[:, :, core], [sibling], deep + wide - 1)
    per = ub_ref.shape[1]
    gain_ref[...] = jnp.concatenate([tiny_all[p][0:1, :shard] for p in places], axis=1)
    bias_ref[...] = jnp.concatenate([tiny_all[p][1:2, :shard] for p in places], axis=1)
    low_b = jnp.concatenate([tiny_all[p][2:3, :per] for p in places[:batch]], axis=1)
    high_b = jnp.concatenate([tiny_all[p][2:3, :per] for p in places[batch:]], axis=1)
    gb_ref[...] = jnp.where(y == 0, low_b, high_b)

    sides = ((tokens, cotan, slice(0, own_rows)), (x_par, dy_par, slice(own_rows, 2 * own_rows)))

    def normalise(side):
        @pl.loop(0, own_rows // STRIP)
        def _(turn):
            strip = pl.ds(pl.multiple_of(turn * STRIP, 16), STRIP)
            vhat, _ = norm_stats(sides[side][0][strip, :].astype(F32))
            normed[pl.ds(pl.multiple_of(side * own_rows + turn * STRIP, 16), STRIP), :] = (vhat * gain_ref[...]).astype(BF)

    def expand(side, at, back):
        rows = sides[side][2]

        turns = 3 if back else 12

        @pl.loop(0, turns)
        def _(turn):
            size = (at.stop - at.start) // turns
            some = pl.ds(pl.multiple_of(at.start + turn * size, LANES), size)
            act[rows, some], slope = gelu_parts(dot(normed[rows, :], weight(0, some)) + gb_ref[:, some])
            if back:
                slope *= dot(sides[side][1][...], weight(1, some))
            d_hid[rows, some] = slope.astype(BF)

    def apply_back(side):
        rows = sides[side][2]

        @pl.loop(0, 2)
        def _(turn):
            at = pl.ds(pl.multiple_of(turn * block, LANES), block)
            d_hid[rows, at] = (d_hid[rows, at].astype(F32) * dot(sides[side][1][...], weight(1, at))).astype(BF)

    def contract(side, low, kept, part):
        rows = sides[side][2]
        size = width // 2

        @pl.loop(0, 2)
        def _(turn):
            if direct:
                value = wires[part][pl.ds(turn * (deep // 2), deep // 2)].reshape(size, hidden)
            else:
                value = flats[part][pl.ds(pl.multiple_of(turn * size, 16), size), :]
            kept[rows, pl.ds(pl.multiple_of(turn * size, LANES), size)] = dot(low[rows, :], value, NT).astype(BF)

    def place_rows(base, ref, values):
        for at in range(own_rows // PATCHES):
            ref[pl.ds(pl.multiple_of((base + at) * SLOT, 16), PATCHES), :] = values[at * PATCHES : (at + 1) * PATCHES].astype(BF)

    def queries_keys():
        ones_low = head_ones()

        @pl.loop(0, 2)
        def _(side):
            rows = pl.ds(pl.multiple_of(side * own_rows, 16), own_rows)
            base = jnp.where(side == 0, y, 1 - y) * (own_rows // PATCHES)
            for at, (raw_ref, low_ref, gain) in enumerate(((s_qraw, s_q, 3), (s_kraw, s_k, 4))):
                raw = dot(normed[rows, :], weight(2, slice(at * cols, (at + 1) * cols)))
                raw_ref[rows, :] = raw.astype(BF)
                hat, _ = head_stats(raw, ones_low)
                place_rows(base, low_ref, hat * repeated(tiny[gain : gain + 1, :HD], cols // HD))

    def values_of():
        @pl.loop(0, 2)
        def _(side):
            rows = pl.ds(pl.multiple_of(side * own_rows, 16), own_rows)
            place_rows(jnp.where(side == 0, y, 1 - y) * (own_rows // PATCHES), s_v, dot(normed[rows, :], weight(2, slice(2 * cols, 3 * cols))))

    def back_of(side):
        place_rows((y if side == 0 else 1 - y) * (own_rows // PATCHES), s_do, dot(sides[side][1][...], weight(2, pl.ds(pl.multiple_of((3 + y) * cols, LANES), cols))))

    over_sib = []

    def grad_own(part):
        rows = sides[0][2]

        @pl.loop(0, 6)
        def _(turn):
            size = hidden // 6
            some = pl.ds(pl.multiple_of(turn * size, LANES), size)
            value = dot(normed[rows, :], d_hid[rows, some], TN) if part == 0 else dot(cotan[...], act[rows, some], TN)
            for b in range(batch):
                grads[part][b // (2 * wide), (b // 2) % wide, b % 2, :, some] = value[b * pair : (b + 1) * pair].astype(BF)

    def grad_rest(part, at):
        rows = sides[1][2]

        @pl.loop(0, 2)
        def _(turn):
            size = (at.stop - at.start) // 2
            some = pl.ds(pl.multiple_of(at.start + turn * size, LANES), size)
            value = dot(normed[rows, :], d_hid[rows, some], TN) if part == 0 else dot(dy_par[...], act[rows, some], TN)
            for b in range(batch):
                block_at = (b // (2 * wide), (b // 2) % wide, b % 2, slice(None), some)
                grads[part][block_at] = (grads[part][block_at].astype(F32) + value[b * pair : (b + 1) * pair]).astype(BF)

        i = len(over_sib)
        over_sib.append(remote(grads[part].at[:, :, 1 - core, :, at], got_core[part].at[:, :, :, at], csend.at[i], crecv.at[i], sibling))
        over_sib[i].start()

    def add_core(i, part, at):
        over_sib[i].wait_recv()

        @pl.loop(0, deep)
        def _(zz):
            for xx in range(wide):
                total = grads[part][zz, xx, core, :, at].astype(F32) + got_core[part][zz, xx, :, at].astype(F32)
                got_core[part][zz, xx, :, at] = total.astype(BF)

    first, second = slice(0, block), slice(block, 2 * block)
    start_x(0)
    normalise(0)
    start_x(1)
    start_core(0)
    start_x(2)
    start_core(1)
    arrive(0)
    arrive(1)
    expand(0, first, True)
    start_x(3)
    start_core(2)
    rows_copy[0].wait_recv()
    normalise(1)
    put(x_par, o_x)
    put(normed, o_normed)
    start_x(4)
    start_core(3)
    arrive(2)
    arrive(3)
    expand(0, second, True)
    start_core(4)
    expand(1, slice(0, hidden), False)
    start_x(5)
    contract(0, act, s_out, 1)
    contract(0, d_hid, s_dn, 0)
    grad_own(0)
    grad_own(1)
    contract(1, act, s_out, 1)
    put(s_out.at[pl.ds(0, own_rows)], o_own)
    put(s_out.at[pl.ds(own_rows, own_rows)], o_other)
    arrive(4)
    start_core(5)
    queries_keys()
    for src, dst in ((s_q, o_q), (s_k, o_k), (s_qraw, o_qraw), (s_kraw, o_kraw)):
        put(src, dst)
    arrive(5)
    put(wires[2] if direct else flats[2], o_heads)
    values_of()
    put(s_v, o_v)
    back_of(0)
    rows_copy[1].wait_recv()
    put(dy_par, o_dy)
    back_of(1)
    put(s_do, o_do)
    apply_back(1)
    contract(1, d_hid, s_dn, 0)
    put(s_dn, o_dn)
    grad_rest(0, first)
    grad_rest(0, second)
    add_core(0, 0, first)
    grad_rest(1, first)
    add_core(1, 0, second)
    for s in range(wide):
        put(got_core[0].at[:, (x + s) % wide], o_sums[0][s])
    grad_rest(1, second)
    add_core(2, 1, first)

    @pl.loop(0, 6)
    def _(turn):
        some = pl.ds(pl.multiple_of(turn * (hidden // 6), LANES), hidden // 6)
        gb_ref[:, some] = dot(jnp.ones((8, 2 * own_rows), BF), d_hid[:, some])[:1]

    add_core(3, 1, second)
    for s in range(wide):
        put(got_core[1].at[:, (x + s) % wide], o_sums[1][s])
    for copy in outs:
        copy.wait()
    for copy in spread_tiny + over_y + rows_copy + [c for group in over_z + over_x for c in group] + over_core + over_sib:
        copy.wait_send()


def first_half(tokens, cotan, weights, vectors, batch):
    deep, wide = grid_of(batch)
    own_rows, width = tokens.shape
    shard, hidden = weights[2].shape[0], weights[2].shape[1] // 2
    cols = hidden // 4
    block = hidden // 2
    rows = 2 * own_rows
    spread_rows = rows // PATCHES * SLOT
    widths = (hidden, hidden, 5 * cols)
    first, second = slice(0, block), slice(block, hidden)
    cuts = [(0, first), (1, first), (0, second), (1, second), (2, slice(0, 2 * cols)), (2, slice(2 * cols, 5 * cols))]
    vm = pl.BlockSpec(memory_space=pltpu.VMEM)
    hbm = pl.BlockSpec(memory_space=pl.ANY)
    direct = (2 * shard) % 16 == 0
    wire_shapes = [(deep, wide, 2, 2 * shard, w) for w in widths]
    flat_shapes = [(width, w) for w in widths]
    low = lambda *shape: jax.ShapeDtypeStruct(shape, BF)
    outs = [low(own_rows, width)] * 2 + [low(rows, width)] + [low(spread_rows, cols)] * 4 + [low(rows, cols)] * 2
    outs += [low(*(wire_shapes if direct else flat_shapes)[2])] + [low(own_rows, width)] * 2 + [low(rows, width)] + [low(deep, 2 * shard, hidden)] * (2 * wide)
    tiny_outs = [jax.ShapeDtypeStruct((1, hidden), F32), jax.ShapeDtypeStruct((1, width), F32), jax.ShapeDtypeStruct((1, width), F32), jax.ShapeDtypeStruct(TINY, F32)]
    buf = lambda *shape: pltpu.VMEM(shape, BF)
    scratch = [buf(2, shard, w) for w in widths] + [buf(shard, w) for w in widths] + [buf(*s) for s in wire_shapes]
    scratch += [buf(*TINY), pltpu.VMEM((deep, wide, 2, 2) + TINY, F32), buf(own_rows, width), buf(own_rows, width), buf(rows, width), buf(rows, hidden), buf(rows, hidden)]
    scratch += [buf(spread_rows, cols)] * 4 + [buf(rows, cols)] * 2 + [buf(rows, width)] * 2
    scratch += [buf(deep, wide, 2, 2 * shard, hidden)] * 2 + [buf(deep, wide, 2 * shard, hidden)] * 2
    scratch += [buf(16, LANES) if direct else buf(*s) for s in flat_shapes]
    scratch += [pltpu.SemaphoreType.DMA((len(cuts), deep + wide))] * 2 + [pltpu.SemaphoreType.DMA((deep + wide + 2,))] * 2 + [pltpu.SemaphoreType.DMA((4,))] * 2 + [pltpu.SemaphoreType.DMA((len(outs),))]
    return pl.pallas_call(
        functools.partial(first_kernel, deep=deep, wide=wide, cuts=cuts, block=block),
        in_specs=[vm] * 11,
        out_specs=[hbm] * len(outs) + [vm] * 4,
        out_shape=outs + tiny_outs,
        scratch_shapes=scratch,
        compiler_params=pltpu.CompilerParams(collective_id=0, has_side_effects=True, vmem_limit_bytes=VMEM_CAP),
        name="gather_and_feed_forward",
    )(tokens, cotan, *weights, *vectors)


def load_rows(ref, block, blocks):
    parts = [ref[pl.ds(pl.multiple_of((block + at) * SLOT, 16), PATCHES), :] for at in range(blocks)]
    return parts[0] if blocks == 1 else jnp.concatenate([p.astype(F32) for p in parts], axis=0).astype(BF)

def attend_pair(pair_q, pair_k, pair_v, pair_do, pieces):
    count = pair_q.shape[0]
    lane = lax.broadcasted_iota(jnp.int32, (count, 2 * HD), 1)
    pair_q = pair_q * jnp.asarray(0.125, BF)
    zero = jnp.zeros_like(pair_q)
    v_t, k_t = pair_v.T, pair_k.T
    mixed, grads_q, grad_k, grad_v = [], [], None, None
    for head in range(2):
        mine = (lane < HD) if head == 0 else (lane >= HD)
        q_m, do_m = jnp.where(mine, pair_q, zero), jnp.where(mine, pair_do, zero)
        part = slice(head * HD, (head + 1) * HD)
        outs, gqs = [], []
        for first, size in pieces:
            q, d_o = q_m[first : first + size], do_m[first : first + size]
            shifted = jnp.exp(dot(pair_k, q, NT))
            total = jnp.sum(shifted, axis=0, keepdims=True)
            weights = shifted * (1.0 / total)
            low = weights.astype(BF)
            d_weights = dot(pair_v, d_o, NT)
            inner = jnp.sum(weights * d_weights, axis=0, keepdims=True)
            d_scores = (weights * (d_weights - inner)).astype(BF)
            outs.append(dot(v_t[part], low))
            gqs.append(dot(k_t[part], d_scores))
            gv, gk = dot(low, d_o), dot(d_scores, q)
            grad_v = gv if grad_v is None else grad_v + gv
            grad_k = gk if grad_k is None else grad_k + gk
        join = lambda parts: parts[0] if len(parts) == 1 else jnp.concatenate(parts, axis=1)
        mixed.append(join(outs))
        grads_q.append(join(gqs))
    turn = lambda parts: jnp.concatenate(parts, axis=0).T
    return turn(mixed), turn(grads_q) * 0.125, grad_k, grad_v

def attention_kernel(count_ref, *refs, pieces, together):
    ins, outs, (small_ref,) = refs[:4], refs[4:8], refs[8:]
    place, smalls, bigs, big_at = 0, 0, 0, 0
    for slot in range(count_ref.shape[0]):
        count = count_ref[slot]
        is_small = (count == PATCHES).astype(jnp.int32)
        is_big = (count == LONGEST).astype(jnp.int32)
        small_ref[smalls] = place
        big_at = jnp.where(is_big == 1, place, big_at)
        smalls, bigs = smalls + is_small, bigs + is_big
        place = place + is_small + (LONGEST // PATCHES) * is_big

    def images(firsts, blocks, pieces):
        loaded = [[load_rows(ref, block, blocks) for ref in ins] for block in firsts]
        results = [attend_pair(*values, pieces) for values in loaded]
        for block, result in zip(firsts, results):
            for ref, values in zip(outs, result):
                for at in range(blocks):
                    ref[pl.ds(pl.multiple_of((block + at) * SLOT, 16), PATCHES), :] = values[at * PATCHES : (at + 1) * PATCHES].astype(ref.dtype)

    @pl.when(bigs > 0)
    def _():
        images([big_at], LONGEST // PATCHES, pieces)

    @pl.loop(0, smalls // together)
    def _(turn):
        images([small_ref[turn * together + at] for at in range(together)], 1, ((0, PATCHES),))

def attention(counts, q, k, v, d_o, pieces=((0, 784),), together=4):
    rows, cols = q.shape
    sm = pl.BlockSpec(memory_space=pltpu.SMEM)
    blk = pl.BlockSpec((rows, 2 * HD), lambda j: (0, j))
    return pl.pallas_call(
        functools.partial(attention_kernel, pieces=pieces, together=together),
        grid=(cols // (2 * HD),),
        in_specs=[sm] + [blk] * 4,
        out_specs=[blk] * 4,
        out_shape=[jax.ShapeDtypeStruct((rows, cols), t) for t in (BF, BF, BF, BF)],
        scratch_shapes=[pltpu.SMEM((counts.shape[0] + 1,), jnp.int32)],
        compiler_params=pltpu.CompilerParams(vmem_limit_bytes=VMEM_CAP),
        cost_estimate=pl.CostEstimate(flops=20_000_000_000, bytes_accessed=20_000_000, transcendentals=rows * LONGEST * cols // HD),
        name="attention",
    )(counts, q, k, v, d_o)


def last_kernel(*refs, deep, wide, cuts):
    tokens, cotan, bias_ref, gb_ref, gains_ref = refs[:5]
    i_x, i_dy, i_normed, i_o, i_dq, i_dk, i_dv, i_qraw, i_kraw, i_heads, i_own, i_got, i_dn = refs[5:18]
    i_sums = (refs[18 : 18 + wide], refs[18 + wide : 18 + 2 * wide])
    o_dn, o_dn_got, block_ref, qkv_ref, wo_ref, up_ref, down_ref, small_ref = refs[18 + 2 * wide : 26 + 2 * wide]
    scratch = refs[26 + 2 * wide :]
    x_par, dy_par, normed, s_o, s_dq, s_dk, s_dv, qraw, kraw, head_w, out_own, out_got, dn = scratch[:13]
    terms = scratch[13:15]
    mine, got_core, got_x = scratch[15:18]
    to_z, got_z, to_y, got_y = (scratch[18 + 3 * i : 21 + 3 * i] for i in range(4))
    d_proj, mixed, o_got = scratch[30:33]
    t_all, t_core, t_x, t_xgot, t_z, t_zgot, t_y, t_ygot = scratch[33:41]
    send, recv, tsend, trecv, lsem, gsem, osem = scratch[41:]
    (z, x, core, y), partner, along_z, along_x, sibling = neighbours(deep, wide)
    batch = 2 * deep * wide
    own_rows, width = tokens.shape
    rows = 2 * own_rows
    cols = qraw.shape[1]
    shard = to_y[0].shape[0]
    slots = own_rows // PATCHES
    places = [(b // (2 * wide), (b // 2) % wide, b % 2, s) for b in range(batch) for s in range(2)]
    own, other = slice(0, own_rows), slice(own_rows, rows)
    greet([partner, sibling] + along_z + along_x)

    theirs = pl.ds(pl.multiple_of((1 - y) * slots * SLOT, 16), slots * SLOT)
    rows_copy = [remote(i_o.at[theirs], o_got, tsend.at[deep + wide], trecv.at[deep + wide], partner)]
    rows_copy[0].start()
    held = {}
    for part in range(2):
        for s in range(wide):
            held[part, s] = pltpu.make_async_copy(i_sums[part][s], terms[part].at[s], gsem.at[part * wide + s])
            held[part, s].start()
    loads = {}
    for at, (name, src, dst) in enumerate((("qraw", i_qraw, qraw), ("dq", i_dq, s_dq), ("kraw", i_kraw, kraw), ("dk", i_dk, s_dk), ("dv", i_dv, s_dv), ("heads", i_heads, head_w), ("dn", i_dn, dn), ("normed", i_normed, normed), ("o", i_o, s_o), ("dy", i_dy, dy_par), ("x", i_x, x_par), ("own", i_own, out_own), ("got", i_got, out_got))):
        loads[name] = pltpu.make_async_copy(src, dst, lsem.at[at])
        loads[name].start()

    first, second, third, fourth = {}, {}, {}, {}

    def over_core(i):
        part, at = cuts[i]
        first[i] = remote(mine.at[:, :, 1 - core, :, at], got_core.at[:, :, :, at], send.at[i, 0], recv.at[i, 0], sibling)
        first[i].start()

    def over_x(i):
        part, at = cuts[i]
        first[i].wait_recv()

        @pl.loop(0, deep)
        def _(zz):
            for xx in range(wide):
                got_core[zz, xx, :, at] = (mine[zz, xx, core, :, at].astype(F32) + got_core[zz, xx, :, at].astype(F32)).astype(BF)

        second[i] = []
        for s, peer in enumerate(along_x):
            copy = remote(got_core.at[:, (x + s + 1) % wide, :, at], got_x.at[s, :, :, at], send.at[i, 1 + s], recv.at[i, 1 + s], peer)
            copy.start()
            second[i].append(copy)

    def over_z(i):
        part, at = cuts[i]
        if part == 2:
            for copy in second[i]:
                copy.wait_recv()

        @pl.loop(0, deep)
        def _(zz):
            if part == 2:
                total = got_core[zz, x, :, at].astype(F32)
                for s in range(wide - 1):
                    total += got_x[s, zz, :, at].astype(F32)
            else:
                total = terms[part][0, zz, :, at].astype(F32)
                for s in range(1, wide):
                    total += terms[part][s, zz, :, at].astype(F32)
            to_z[part][zz, :, at] = total.astype(BF)

        third[i] = []
        for s, peer in enumerate(along_z):
            copy = remote(to_z[part].at[(z + s + 1) % deep, :, at], got_z[part].at[s, :, at], send.at[i, wide + s], recv.at[i, wide + s], peer)
            copy.start()
            third[i].append(copy)

    def over_y(i):
        part, at = cuts[i]
        for copy in third[i]:
            copy.wait_recv()
        total = to_z[part][z, :, at].astype(F32)
        for s in range(deep - 1):
            total += got_z[part][s, :, at].astype(F32)
        low, high = total[:shard], total[shard:]
        to_y[part][:, at] = jnp.where(y == 0, high, low).astype(BF)
        fourth[i] = remote(to_y[part].at[:, at], got_y[part].at[:, at], send.at[i, wide + deep - 1], recv.at[i, wide + deep - 1], partner)
        fourth[i].start()
        deliver(part, y, at, jnp.where(y == 0, low, high))

    def deliver(part, half, at, values):
        if part < 2:
            ref = (up_ref, down_ref)[part]
            ref[:, pl.ds(pl.multiple_of(half * 4 * cols + at.start, LANES), at.stop - at.start)] = values
            return
        for piece in range(at.start // cols, at.stop // cols):
            some = values[:, piece * cols - at.start : (piece + 1) * cols - at.start]
            lanes = pl.ds(pl.multiple_of(half * cols, LANES), cols)
            if piece < 3:
                qkv_ref[piece, :, lanes] = some
            else:
                wo_ref[:, lanes] = some

    def last(i):
        part, at = cuts[i]
        fourth[i].wait_recv()
        deliver(part, 1 - y, at, got_y[part][:, at].astype(F32))

    def compact_rows(ref, base):
        parts = [ref[pl.ds(pl.multiple_of((base + at) * SLOT, 16), PATCHES), :].astype(F32) for at in range(slots)]
        return jnp.concatenate(parts, axis=0)

    bases = (y * slots, (1 - y) * slots)

    def head_rows(turn, at):
        if len(head_w.shape) > 2:
            value = head_w[pl.ds(turn * (deep // 2), deep // 2), :, :, :, at]
            return value.reshape(width // 2, value.shape[-1])
        return head_w[pl.ds(pl.multiple_of(turn * (width // 2), 16), width // 2), at]

    for part in range(2):
        for s in range(wide):
            held[part, s].wait()
    for i in range(4):
        over_z(i)
    ones_low = head_ones()
    gains = []
    for names, grad_in, raw_ref, gain, at in ((("dq", "qraw"), s_dq, qraw, 3, 0), (("dk", "kraw"), s_dk, kraw, 4, 1)):
        for name in names:
            loads[name].wait()

        def one_side(side, total):
            part = pl.ds(pl.multiple_of(side * own_rows, 16), own_rows)
            hat, scale = head_stats(raw_ref[part, :].astype(F32), ones_low)
            grad = compact_rows(grad_in, jnp.where(side == 0, *bases))
            scaled = grad * repeated(gains_ref[gain : gain + 1, :HD], cols // HD)
            d_raw = (scaled - head_means(scaled, ones_low) - hat * head_means(scaled * hat, ones_low)) * scale
            d_proj[part, at * cols : (at + 1) * cols] = d_raw.astype(BF)
            return total + jnp.sum(grad * hat, axis=0, keepdims=True)

        total = lax.fori_loop(0, 2, one_side, jnp.zeros((1, cols), F32))
        folded = total[:, :HD]
        for head in range(1, cols // HD):
            folded += total[:, head * HD : (head + 1) * HD]
        gains.append(folded)
    loads["dv"].wait()

    @pl.loop(0, 2)
    def _(side):
        d_proj[pl.ds(pl.multiple_of(side * own_rows, 16), own_rows), 2 * cols : 3 * cols] = compact_rows(s_dv, jnp.where(side == 0, *bases)).astype(BF)

    loads["dn"].wait()
    loads["heads"].wait()

    def add_dn(part):
        size = width // 2

        @pl.loop(0, 2)
        def _(turn):
            some = pl.ds(pl.multiple_of(turn * size, LANES), size)
            dn[part, some] = (dn[part, some].astype(F32) + dot(d_proj[part, :], head_rows(turn, slice(0, 3 * cols)), NT)).astype(BF)

    add_dn(other)
    rows_copy.append(remote(dn.at[pl.ds(own_rows, own_rows)], o_dn_got, tsend.at[deep + wide + 1], trecv.at[deep + wide + 1], partner))
    rows_copy[1].start()

    def keep(at, values):
        for b in range(batch):
            mine[b // (2 * wide), (b // 2) % wide, b % 2, :, at] = values[2 * b * shard : 2 * (b + 1) * shard].astype(BF)

    loads["normed"].wait()

    @pl.loop(0, 3)
    def _(piece):
        at = pl.ds(pl.multiple_of(piece * cols, LANES), cols)
        keep(at, dot(normed[...], d_proj[:, at], TN))

    over_core(4)
    loads["o"].wait()
    loads["dy"].wait()

    @pl.loop(0, 2)
    def _(side):
        mixed[pl.ds(pl.multiple_of(side * own_rows, 16), own_rows), :] = compact_rows(s_o, jnp.where(side == 0, *bases)).astype(BF)

    over_y(0)
    over_x(4)
    keep(slice(3 * cols, 4 * cols), dot(cotan[...], mixed[own, :], TN) + dot(dy_par[...], mixed[other, :], TN))
    over_core(5)
    add_dn(own)
    puts = [pltpu.make_async_copy(dn.at[pl.ds(0, own_rows)], o_dn, osem)]
    puts[0].start()
    over_x(5)
    over_y(1)
    loads["x"].wait()
    grad_g = jnp.zeros((1, width), F32)
    for side, ref in enumerate((tokens, x_par)):

        def one_strip(turn, total):
            vhat, _ = norm_stats(ref[pl.ds(pl.multiple_of(turn * STRIP, 16), STRIP), :].astype(F32))
            some = dn[pl.ds(pl.multiple_of(side * own_rows + turn * STRIP, 16), STRIP), :].astype(F32)
            return total + jnp.sum(some * vhat, axis=0, keepdims=True)

        grad_g = lax.fori_loop(0, own_rows // STRIP, one_strip, grad_g)

    def add_strip(turn, total):
        return total + jnp.sum(cotan[pl.ds(pl.multiple_of(turn * STRIP, 16), STRIP), :].astype(F32), axis=0, keepdims=True)

    grad_db = lax.fori_loop(0, own_rows // STRIP, add_strip, jnp.zeros((1, width), F32))
    per = gb_ref.shape[1] // batch
    both = jnp.concatenate(gains, axis=1)
    bias = gb_ref[...]
    t_all[...] = jnp.zeros(t_all.shape, F32)
    for b, (zz, xx, cc, s) in enumerate(places):
        inside = jnp.where(y == b // batch, 1.0, 0.0)
        t_all[zz, xx, cc, s, 0:1, :shard] = grad_g[:, b * shard : (b + 1) * shard]
        t_all[zz, xx, cc, s, 1:2, :shard] = grad_db[:, b * shard : (b + 1) * shard]
        t_all[zz, xx, cc, s, 2:3, :per] = bias[:, (b % batch) * per : (b % batch + 1) * per] * inside
        t_all[zz, xx, cc, s, 3:4, : 2 * HD] = both
    tiny = [remote(t_all.at[:, :, 1 - core], t_core, tsend.at[0], trecv.at[0], sibling)]
    tiny[0].start()
    for name in ("own", "got"):
        loads[name].wait()
    rows_copy[0].wait_recv()
    mixed_got = compact_rows(o_got, 0).astype(BF)
    mixed_own = mixed[own, :]
    all_heads = jnp.concatenate([jnp.where(y == 0, mixed_own, mixed_got), jnp.where(y == 0, mixed_got, mixed_own)], axis=1)

    @pl.loop(0, 2)
    def _(turn):
        some = pl.ds(pl.multiple_of(turn * (width // 2), LANES), width // 2)
        attended = dot(all_heads, head_rows(turn, slice(3 * cols, 5 * cols)), NT)
        block_ref[:, some] = (tokens[:, some].astype(F32) + attended + out_own[:, some].astype(F32) + out_got[:, some].astype(F32) + bias_ref[:, some]).astype(BF)

    tiny[0].wait_recv()
    t_x[...] = t_all[:, :, core] + t_core[...]
    group = []
    for s, peer in enumerate(along_x):
        group.append(remote(t_x.at[:, (x + s + 1) % wide], t_xgot.at[x], tsend.at[1 + s], trecv.at[1 + s], peer))
        group[s].start()
    tiny += group
    t_xgot[x] = t_x[:, x]
    over_y(2)
    over_z(4)
    for copy in group:
        copy.wait_recv()
    total = t_xgot[0]
    for xx in range(1, wide):
        total += t_xgot[xx]
    t_z[...] = total
    group = []
    for s, peer in enumerate(along_z):
        group.append(remote(t_z.at[(z + s + 1) % deep], t_zgot.at[z], tsend.at[wide + s], trecv.at[wide + s], peer))
        group[s].start()
    tiny += group
    t_zgot[z] = t_z[z]
    over_y(3)
    over_z(5)
    for copy in group:
        copy.wait_recv()
    total = t_zgot[0]
    for zz in range(1, deep):
        total += t_zgot[zz]
    t_y[...] = total
    tiny.append(remote(t_y.at[1 - y], t_ygot, tsend.at[wide + deep - 1], trecv.at[wide + deep - 1], partner))
    tiny[-1].start()
    for i in range(4):
        last(i)
    over_y(4)
    tiny[-1].wait_recv()
    small_ref[...] = t_y[y] + t_ygot[...]
    over_y(5)
    last(4)
    last(5)
    puts[0].wait()
    rows_copy[1].wait_recv()
    for copy in list(first.values()) + [c for group in list(second.values()) + list(third.values()) for c in group] + list(fourth.values()) + tiny + rows_copy:
        copy.wait_send()


def last_half(tokens, cotan, bias, gb, gains, kept, sums, batch):
    deep, wide = grid_of(batch)
    own_rows, width = tokens.shape
    rows = 2 * own_rows
    hidden = gb.shape[1]
    cols = hidden // 4
    block = hidden // 2
    shard = width // (2 * batch)
    slots = own_rows // PATCHES
    cuts = [(part, slice(at, at + block)) for part in range(3) for at in (0, block)]
    vm = pl.BlockSpec(memory_space=pltpu.VMEM)
    hbm = pl.BlockSpec(memory_space=pl.ANY)
    buf = lambda *shape: pltpu.VMEM(shape, BF)
    tile = lambda *lead: pltpu.VMEM(lead + TINY, F32)
    scratch = [buf(*k.shape) for k in kept]
    scratch += [buf(wide, deep, 2 * shard, hidden)] * 2
    scratch += [buf(deep, wide, 2, 2 * shard, hidden), buf(deep, wide, 2 * shard, hidden), buf(wide - 1, deep, 2 * shard, hidden)]
    scratch += [buf(deep, 2 * shard, hidden)] * 3 + [buf(deep - 1, 2 * shard, hidden)] * 3 + [buf(shard, hidden)] * 6
    scratch += [buf(rows, 3 * cols), buf(rows, cols), buf(slots * SLOT, cols)]
    scratch += [tile(deep, wide, 2, 2), tile(deep, wide, 2), tile(deep, wide, 2), tile(wide, deep, 2), tile(deep, 2), tile(deep, 2), tile(2), tile()]
    scratch += [pltpu.SemaphoreType.DMA((len(cuts), deep + wide))] * 2 + [pltpu.SemaphoreType.DMA((deep + wide + 2,))] * 2 + [pltpu.SemaphoreType.DMA((len(kept),)), pltpu.SemaphoreType.DMA((2 * wide,)), pltpu.SemaphoreType.DMA]
    full = lambda *shape: jax.ShapeDtypeStruct(shape, F32)
    low = jax.ShapeDtypeStruct((own_rows, width), BF)
    return pl.pallas_call(
        functools.partial(last_kernel, deep=deep, wide=wide, cuts=cuts),
        in_specs=[vm] * 5 + [hbm] * (len(kept) + 2 * wide),
        out_specs=[hbm] * 2 + [vm] * 6,
        out_shape=[low] * 3 + [full(3, shard, 2 * cols), full(shard, 2 * cols), full(shard, 2 * hidden), full(shard, 2 * hidden), full(*TINY)],
        scratch_shapes=scratch,
        compiler_params=pltpu.CompilerParams(collective_id=1, has_side_effects=True, vmem_limit_bytes=VMEM_CAP),
        name="head_gradients_and_scatter",
    )(tokens, cotan, bias, gb, gains, *kept, *sums)


def result_kernel(tokens, cotan, gain, dn_own, dn_got, block_in, qkv_in, wo_in, up_in, down_in, small, block, grad, qkv, wo, up, down, up_b, down_b, norm_g, query_g, key_g):
    vhat, scale = norm_stats(tokens[...].astype(F32))
    scaled = (dn_own[...].astype(F32) + dn_got[...].astype(F32)) * gain[...]
    d_tokens = (scaled - jnp.mean(scaled, axis=-1, keepdims=True) - vhat * jnp.mean(scaled * vhat, axis=-1, keepdims=True)) * scale
    grad[...] = (cotan[...].astype(F32) + d_tokens).astype(BF)
    block[...] = block_in[...]

    @pl.when(pl.program_id(0) == 0)
    def _():
        qkv[...] = qkv_in[...]
        wo[...] = wo_in[...]
        up[...] = up_in[...]
        down[...] = down_in[...]
        norm_g[...] = small[0:1, : norm_g.shape[1]]
        down_b[...] = small[1:2, : down_b.shape[1]]
        up_b[...] = small[2:3, : up_b.shape[1]]
        query_g[...] = small[3:4, :HD]
        key_g[...] = small[3:4, HD : 2 * HD]


def results(tokens, cotan, gain, dn_own, dn_got, block_in, sums, small, per):
    rows, width = tokens.shape
    chunk = rows // 2
    shard = sums[1].shape[0]
    blk = pl.BlockSpec((chunk, width), lambda j: (j, 0))
    whole = lambda shape: pl.BlockSpec(shape, lambda j: (0,) * len(shape))
    vectors = [(1, per), (1, shard), (1, shard), (1, HD), (1, HD)]
    return pl.pallas_call(
        result_kernel,
        grid=(rows // chunk,),
        in_specs=[blk, blk, whole(gain.shape), blk, blk, blk] + [whole(s.shape) for s in sums] + [whole(small.shape)],
        out_specs=[blk, blk] + [whole(s.shape) for s in sums] + [whole(v) for v in vectors],
        out_shape=[jax.ShapeDtypeStruct((rows, width), BF)] * 2 + [jax.ShapeDtypeStruct(s.shape, F32) for s in sums] + [jax.ShapeDtypeStruct(v, F32) for v in vectors],
        compiler_params=pltpu.CompilerParams(vmem_limit_bytes=VMEM_CAP),
        name="results",
    )(tokens, cotan, gain, dn_own, dn_got, block_in, *sums, small)


def local(tokens, cotangent, image_tokens, w_qkv, w_out, w_up, bias_up, w_down, bias_down, norm_gain, query_gain, key_gain):
    batch = lax.axis_size("batch")
    deep, wide = grid_of(batch)
    row = lambda v: v.reshape(1, -1)
    weights = (w_qkv, w_out.T, w_up, w_down.T)
    vectors = (row(norm_gain), row(bias_down), row(bias_up), row(query_gain), row(key_gain))
    made = first_half(tokens, cotangent, weights, vectors, batch)
    x_par, dy_par, normed, q, k, v, d_o, qraw, kraw, head_w, out_own, out_other, dn = made[:13]
    up_sums, down_sums = made[13 : 13 + wide], made[13 + wide : 13 + 2 * wide]
    gb, gain, bias, gains = made[13 + 2 * wide :]
    at = lambda z, x, c: (z * wide + x) * 2 + c

    def over_x(terms):
        return [terms[0]] + [lax.ppermute(terms[s], "batch", [(at(z, x, c), at(z, (x + s) % wide, c)) for z in range(deep) for x in range(wide) for c in range(2)]) for s in range(1, wide)]

    up_sums = over_x(up_sums)
    out_got = lax.ppermute(out_other, "branch", [(0, 1), (1, 0)])
    down_sums = over_x(down_sums)
    o, dq, dk, dv = attention(image_tokens[0], q, k, v, d_o)
    kept = [x_par, dy_par, normed, o, dq, dk, dv, qraw, kraw, head_w, out_own, out_got, dn]
    dn_own, dn_got, block_in, g_qkv, g_out, g_up, g_down, small = last_half(tokens, cotangent, bias, gb, gains, kept, up_sums + down_sums, batch)
    block_out, grad_tokens, g_qkv, g_out, g_up, g_down, g_up_b, g_down_b, g_norm, g_query, g_key = results(tokens, cotangent, gain, dn_own, dn_got, block_in, [g_qkv, g_out, g_up, g_down], small, bias_up.shape[0])
    flat = lambda v: v.reshape(-1)
    return (block_out, grad_tokens, g_qkv, g_out.T, g_up, flat(g_up_b), g_down.T, flat(g_down_b), flat(g_norm), flat(g_query), flat(g_key))


def solution(mesh):
    both = ("batch", "branch")
    in_specs = (P(both, None), P(both, None), P("batch", None), P(None, both, None), P(None, both), P(both, None), P(both), P(None, both), P(both), P(both), P(), P())
    out_specs = (P(both, None), P(both, None), P(None, both, None), P(None, both), P(both, None), P(both), P(None, both), P(both), P(both), P(), P())
    return jax.shard_map(local, mesh=mesh, in_specs=in_specs, out_specs=out_specs, check_vma=False)
```

profile of v0, /device:TPU:0, one launch (start us, length us, event | category | flops | bytes accessed | tf_op | source)
XLA Modules:
  0.0 202.9 jit_solution(16706840430222157499)
XLA Ops:
  0.6 108.7 %gather_and_feed_forward.1 = (bf16[784,768]{1,0:T(8,128)(2,1)}, bf16[784,768]{1,0:T(8,128)(2,1)}, bf16[1568,768]{1,0:T(8,128)(2,1)}, bf16[1664,384]{1,0:T(8,128)...) custom-call(bf16[784,768]{1,0:T(8,128)(2,1)} %tokens.1, ...), custom_call_target="tpu_custom_call" | custom-call | tf_op jit(solution)/shard_map/gather_and_feed_forward/pallas_call | solution.py:433
  109.3 0.8 collective-permute-start.1
  110.1 1.3 collective-permute-start.2
  111.4 0.7 collective-permute-start
  112.2 27.3 %attention.1 = (bf16[1664,384]{1,0:T(8,128)(2,1)}, bf16[1664,384]{1,0:T(8,128)(2,1)}, bf16[1664,384]{1,0:T(8,128)(2,1)}, bf16[1664,384]{1,0:T(8,128)(2,1)}) custom-call(s32[8]{0:T(128)} %bitcast.24, bf16[1664,384]{1,0:T(8,128)(2,1)} %get-tuple-element.62.refs_0_, bf16[1664,384]{1,0:T(8,128)(2,1)} %get-tuple-element.63.refs_1_, ...), custom_call_target="tpu_custom_call" | custom-call | flops 20000000000 | bytes 20000000 | tf_op jit(solution)/shard_map/attention/pallas_call | solution.py:512
  139.5 0.0 collective-permute-done.1.refs_19_
  139.5 0.0 copy-start
  139.5 0.0 collective-permute-done.2.refs_21_
  139.5 0.4 collective-permute-done.refs_16_
  139.9 0.4 copy-done
  140.3 56.6 %head_gradients_and_scatter.1 = (bf16[784,768]{1,0:T(8,128)(2,1)}, bf16[784,768]{1,0:T(8,128)(2,1)}, bf16[784,768]{1,0:T(8,128)(2,1)}, f32[3,24,768]{2,1,0:T(8,1...) custom-call(bf16[784,768]{1,0:T(8,128)(2,1)} %tokens.1, ...), custom_call_target="tpu_custom_call" | custom-call | tf_op jit(solution)/shard_map/head_gradients_and_scatter/pallas_call | solution.py:834
  196.9 5.8 %results.1 = (bf16[784,768]{1,0:T(8,128)(2,1)}, bf16[784,768]{1,0:T(8,128)(2,1)}, f32[3,24,768]{2,1,0:T(8,128)}, f32[24,768]{1,0:T(8,128)}, f32[24,3072]{1,0:T(8...) custom-call(bf16[784,768]{1,0:T(8,128)(2,1)} %tokens.1, ...), custom_call_target="tpu_custom_call" | custom-call | tf_op jit(solution)/shard_map/results/pallas_call | solution.py:872
Async XLA Ops:
  109.3 30.1 %collective-permute-start.1 = (bf16[4,48,1536]{2,1,0:T(8,128)(2,1)}, bf16[4,48,1536]{2,1,0:T(8,128)(2,1)S(1)}, u32[]{:S(2)}, u32[]{:S(2)}) collective-permute-start(bf16[4,48,1536]{2,1,0:T(8,128)(2,1)} %get-tuple-element.77), channel_id=1, source_target_pairs={{0,4},{2,6},{4,0},{6,2},{8,12},{10,14},{12,8},{14,10},{16,20},{18,... | collective-permute-start | bytes 1769480 | tf_op jit(solution)/shard_map/ppermute | solution.py:896
  110.1 29.4 %collective-permute-start.2 = (bf16[4,48,1536]{2,1,0:T(8,128)(2,1)}, bf16[4,48,1536]{2,1,0:T(8,128)(2,1)}, u32[]{:S(2)}, u32[]{:S(2)}) collective-permute-start(bf16[4,48,1536]{2,1,0:T(8,128)(2,1)} %get-tuple-element.79), channel_id=1, source_target_pairs={{0,4},{2,6},{4,0},{6,2},{8,12},{10,14},{12,8},{14,10},{16,20},{18,... | collective-permute-start | bytes 1769480 | tf_op jit(solution)/shard_map/ppermute | solution.py:896
  111.4 28.5 %collective-permute-start = (bf16[784,768]{1,0:T(8,128)(2,1)}, bf16[784,768]{1,0:T(8,128)(2,1)}, u32[]{:S(2)}, u32[]{:S(2)}) collective-permute-start(bf16[784,768]{1,0:T(8,128)(2,1)} %get-tuple-element.74), channel_id=1, source_target_pairs={{0,1},{1,0},{2,3},{3,2},{4,5},{5,4},{6,7},{7,6},{8,9},{9,8},{10,11... | collective-permute-start | bytes 3612680 | tf_op jit(solution)/shard_map/ppermute | solution.py:899
  139.5 0.8 copy-start
where the time goes:
time: 203 us
  Pallas kernels  198 us (98%)
  starting transfers between devices  2.84 us (1%)
    pallas_call x1, Pallas kernels, first_half(): pl.pallas_call(functools.partial(first_kernel, deep=deep, wide=wide, cuts...  109 us
    pallas_call x1, Pallas kernels, last_half(): pl.pallas_call(functools.partial(last_kernel, deep=deep, wide=wide, cuts=...  56.6 us
    pallas_call x1, Pallas kernels, attention(): pl.pallas_call(functools.partial(attention_kernel, pieces=pieces, togethe...  27.3 us
    pallas_call x1, Pallas kernels, results(): pl.pallas_call(result_kernel, grid=(rows // chunk,), in_specs=[blk, blk,...  5.78 us
  transfers between devices with their start and end apart: 3, of which 1 were waited for; matrix products, arithmetic and copies ran while one was open for 0% of the time, Pallas kernels for 13%

commit v1 on v0

--- a/solution.py
+++ b/solution.py
@@ -356,18 +356,21 @@
     expand(1, slice(0, hidden), False)
     start_x(5)
     contract(0, act, s_out, 1)
+    start_x(6)
     contract(0, d_hid, s_dn, 0)
     grad_own(0)
+    start_core(5)
     grad_own(1)
     contract(1, act, s_out, 1)
     put(s_out.at[pl.ds(0, own_rows)], o_own)
     put(s_out.at[pl.ds(own_rows, own_rows)], o_other)
     arrive(4)
-    start_core(5)
+    start_core(6)
     queries_keys()
     for src, dst in ((s_q, o_q), (s_k, o_k), (s_qraw, o_qraw), (s_kraw, o_kraw)):
         put(src, dst)
     arrive(5)
+    arrive(6)
     put(wires[2] if direct else flats[2], o_heads)
     values_of()
     put(s_v, o_v)
@@ -413,7 +416,7 @@
     spread_rows = rows // PATCHES * SLOT
     widths = (hidden, hidden, 5 * cols)
     first, second = slice(0, block), slice(block, hidden)
-    cuts = [(0, first), (1, first), (0, second), (1, second), (2, slice(0, 2 * cols)), (2, slice(2 * cols, 5 * cols))]
+    cuts = [(0, first), (1, first), (0, second), (1, second), (2, slice(0, 2 * cols)), (2, slice(3 * cols, 5 * cols)), (2, slice(2 * cols, 3 * cols))]
     vm = pl.BlockSpec(memory_space=pltpu.VMEM)
     hbm = pl.BlockSpec(memory_space=pl.ANY)
     direct = (2 * shard) % 16 == 0

time: 203 us -> 204 us (level)
  no operation moved by 1% of the time
where the time goes in v1:
time: 204 us
  Pallas kernels  199 us (98%)
  starting transfers between devices  2.87 us (1%)
    pallas_call x1, Pallas kernels, first_half(): pl.pallas_call(functools.partial(first_kernel, deep=deep, wide=wide, cuts...  109 us
    pallas_call x1, Pallas kernels, last_half(): pl.pallas_call(functools.partial(last_kernel, deep=deep, wide=wide, cuts=...  57.1 us
    pallas_call x1, Pallas kernels, attention(): pl.pallas_call(functools.partial(attention_kernel, pieces=pieces, togethe...  27.3 us
    pallas_call x1, Pallas kernels, results(): pl.pallas_call(result_kernel, grid=(rows // chunk,), in_specs=[blk, blk,...  5.78 us
  transfers between devices with their start and end apart: 3, of which 1 were waited for; matrix products, arithmetic and copies ran while one was open for 0% of the time, Pallas kernels for 13%

profile of v1, /device:TPU:0, one launch (start us, length us, event | category | flops | bytes accessed | tf_op | source)
XLA Modules:
  0.0 203.6 jit_solution(1840902021400483843)
XLA Ops:
  0.6 108.8 %gather_and_feed_forward.1 = (bf16[784,768]{1,0:T(8,128)(2,1)}, bf16[784,768]{1,0:T(8,128)(2,1)}, bf16[1568,768]{1,0:T(8,128)(2,1)}, bf16[1664,384]{1,0:T(8,128)...) custom-call(bf16[784,768]{1,0:T(8,128)(2,1)} %tokens.1, ...), custom_call_target="tpu_custom_call" | custom-call | tf_op jit(solution)/shard_map/gather_and_feed_forward/pallas_call | solution.py:436
  109.5 0.8 collective-permute-start.1
  110.3 1.3 collective-permute-start.2
  111.6 0.8 collective-permute-start
  112.3 27.3 %attention.1 = (bf16[1664,384]{1,0:T(8,128)(2,1)}, bf16[1664,384]{1,0:T(8,128)(2,1)}, bf16[1664,384]{1,0:T(8,128)(2,1)}, bf16[1664,384]{1,0:T(8,128)(2,1)}) custom-call(s32[8]{0:T(128)} %bitcast.24, bf16[1664,384]{1,0:T(8,128)(2,1)} %get-tuple-element.62.refs_0_, bf16[1664,384]{1,0:T(8,128)(2,1)} %get-tuple-element.63.refs_1_, ...), custom_call_target="tpu_custom_call" | custom-call | flops 20000000000 | bytes 20000000 | tf_op jit(solution)/shard_map/attention/pallas_call | solution.py:515
  139.7 0.0 collective-permute-done.1.refs_19_
  139.7 0.0 copy-start
  139.7 0.0 collective-permute-done.2.refs_21_
  139.7 0.4 collective-permute-done.refs_16_
  140.1 0.4 copy-done
  140.5 57.1 %head_gradients_and_scatter.1 = (bf16[784,768]{1,0:T(8,128)(2,1)}, bf16[784,768]{1,0:T(8,128)(2,1)}, bf16[784,768]{1,0:T(8,128)(2,1)}, f32[3,24,768]{2,1,0:T(8,1...) custom-call(bf16[784,768]{1,0:T(8,128)(2,1)} %tokens.1, ...), custom_call_target="tpu_custom_call" | custom-call | tf_op jit(solution)/shard_map/head_gradients_and_scatter/pallas_call | solution.py:837
  197.6 5.8 %results.1 = (bf16[784,768]{1,0:T(8,128)(2,1)}, bf16[784,768]{1,0:T(8,128)(2,1)}, f32[3,24,768]{2,1,0:T(8,128)}, f32[24,768]{1,0:T(8,128)}, f32[24,3072]{1,0:T(8...) custom-call(bf16[784,768]{1,0:T(8,128)(2,1)} %tokens.1, ...), custom_call_target="tpu_custom_call" | custom-call | tf_op jit(solution)/shard_map/results/pallas_call | solution.py:875
Async XLA Ops:
  109.5 30.2 %collective-permute-start.1 = (bf16[4,48,1536]{2,1,0:T(8,128)(2,1)}, bf16[4,48,1536]{2,1,0:T(8,128)(2,1)S(1)}, u32[]{:S(2)}, u32[]{:S(2)}) collective-permute-start(bf16[4,48,1536]{2,1,0:T(8,128)(2,1)} %get-tuple-element.77), channel_id=1, source_target_pairs={{0,4},{2,6},{4,0},{6,2},{8,12},{10,14},{12,8},{14,10},{16,20},{18,... | collective-permute-start | bytes 1769480 | tf_op jit(solution)/shard_map/ppermute | solution.py:899
  110.3 29.4 %collective-permute-start.2 = (bf16[4,48,1536]{2,1,0:T(8,128)(2,1)}, bf16[4,48,1536]{2,1,0:T(8,128)(2,1)}, u32[]{:S(2)}, u32[]{:S(2)}) collective-permute-start(bf16[4,48,1536]{2,1,0:T(8,128)(2,1)} %get-tuple-element.79), channel_id=1, source_target_pairs={{0,4},{2,6},{4,0},{6,2},{8,12},{10,14},{12,8},{14,10},{16,20},{18,... | collective-permute-start | bytes 1769480 | tf_op jit(solution)/shard_map/ppermute | solution.py:899
  111.6 28.5 %collective-permute-start = (bf16[784,768]{1,0:T(8,128)(2,1)}, bf16[784,768]{1,0:T(8,128)(2,1)}, u32[]{:S(2)}, u32[]{:S(2)}) collective-permute-start(bf16[784,768]{1,0:T(8,128)(2,1)} %get-tuple-element.74), channel_id=1, source_target_pairs={{0,1},{1,0},{2,3},{3,2},{4,5},{5,4},{6,7},{7,6},{8,9},{9,8},{10,11... | collective-permute-start | bytes 3612680 | tf_op jit(solution)/shard_map/ppermute | solution.py:902
  139.7 0.8 copy-start

commit v2 on v0

--- a/solution.py
+++ b/solution.py
@@ -377,8 +377,6 @@
     back_of(1)
     put(s_do, o_do)
     apply_back(1)
-    contract(1, d_hid, s_dn, 0)
-    put(s_dn, o_dn)
     grad_rest(0, first)
     grad_rest(0, second)
     add_core(0, 0, first)
@@ -387,6 +385,8 @@
     for s in range(wide):
         put(got_core[0].at[:, (x + s) % wide], o_sums[0][s])
     grad_rest(1, second)
+    contract(1, d_hid, s_dn, 0)
+    put(s_dn, o_dn)
     add_core(2, 1, first)
 
     @pl.loop(0, 6)

time: 203 us -> 203 us (level)
  no operation moved by 1% of the time
where the time goes in v2:
time: 203 us
  Pallas kernels  198 us (98%)
  starting transfers between devices  2.87 us (1%)
    pallas_call x1, Pallas kernels, first_half(): pl.pallas_call(functools.partial(first_kernel, deep=deep, wide=wide, cuts...  109 us
    pallas_call x1, Pallas kernels, last_half(): pl.pallas_call(functools.partial(last_kernel, deep=deep, wide=wide, cuts=...  56.6 us
    pallas_call x1, Pallas kernels, attention(): pl.pallas_call(functools.partial(attention_kernel, pieces=pieces, togethe...  27.3 us
    pallas_call x1, Pallas kernels, results(): pl.pallas_call(result_kernel, grid=(rows // chunk,), in_specs=[blk, blk,...  5.78 us
  transfers between devices with their start and end apart: 3, of which 1 were waited for; matrix products, arithmetic and copies ran while one was open for 0% of the time, Pallas kernels for 13%

profile of v2, /device:TPU:0, one launch (start us, length us, event | category | flops | bytes accessed | tf_op | source)
XLA Modules:
  0.0 202.8 jit_solution(10416839362975213554)
XLA Ops:
  0.6 108.5 %gather_and_feed_forward.1 = (bf16[784,768]{1,0:T(8,128)(2,1)}, bf16[784,768]{1,0:T(8,128)(2,1)}, bf16[1568,768]{1,0:T(8,128)(2,1)}, bf16[1664,384]{1,0:T(8,128)...) custom-call(bf16[784,768]{1,0:T(8,128)(2,1)} %tokens.1, ...), custom_call_target="tpu_custom_call" | custom-call | tf_op jit(solution)/shard_map/gather_and_feed_forward/pallas_call | solution.py:433
  109.2 0.8 collective-permute-start.1
  110.0 1.3 collective-permute-start.2
  111.3 0.8 collective-permute-start
  112.1 27.3 %attention.1 = (bf16[1664,384]{1,0:T(8,128)(2,1)}, bf16[1664,384]{1,0:T(8,128)(2,1)}, bf16[1664,384]{1,0:T(8,128)(2,1)}, bf16[1664,384]{1,0:T(8,128)(2,1)}) custom-call(s32[8]{0:T(128)} %bitcast.24, bf16[1664,384]{1,0:T(8,128)(2,1)} %get-tuple-element.62.refs_0_, bf16[1664,384]{1,0:T(8,128)(2,1)} %get-tuple-element.63.refs_1_, ...), custom_call_target="tpu_custom_call" | custom-call | flops 20000000000 | bytes 20000000 | tf_op jit(solution)/shard_map/attention/pallas_call | solution.py:512
  139.4 0.0 collective-permute-done.1.refs_19_
  139.4 0.0 copy-start
  139.4 0.0 collective-permute-done.2.refs_21_
  139.4 0.2 collective-permute-done.refs_16_
  139.6 0.6 copy-done
  140.2 56.6 %head_gradients_and_scatter.1 = (bf16[784,768]{1,0:T(8,128)(2,1)}, bf16[784,768]{1,0:T(8,128)(2,1)}, bf16[784,768]{1,0:T(8,128)(2,1)}, f32[3,24,768]{2,1,0:T(8,1...) custom-call(bf16[784,768]{1,0:T(8,128)(2,1)} %tokens.1, ...), custom_call_target="tpu_custom_call" | custom-call | tf_op jit(solution)/shard_map/head_gradients_and_scatter/pallas_call | solution.py:834
  196.8 5.8 %results.1 = (bf16[784,768]{1,0:T(8,128)(2,1)}, bf16[784,768]{1,0:T(8,128)(2,1)}, f32[3,24,768]{2,1,0:T(8,128)}, f32[24,768]{1,0:T(8,128)}, f32[24,3072]{1,0:T(8...) custom-call(bf16[784,768]{1,0:T(8,128)(2,1)} %tokens.1, ...), custom_call_target="tpu_custom_call" | custom-call | tf_op jit(solution)/shard_map/results/pallas_call | solution.py:872
Async XLA Ops:
  109.2 30.2 %collective-permute-start.1 = (bf16[4,48,1536]{2,1,0:T(8,128)(2,1)}, bf16[4,48,1536]{2,1,0:T(8,128)(2,1)S(1)}, u32[]{:S(2)}, u32[]{:S(2)}) collective-permute-start(bf16[4,48,1536]{2,1,0:T(8,128)(2,1)} %get-tuple-element.77), channel_id=1, source_target_pairs={{0,4},{2,6},{4,0},{6,2},{8,12},{10,14},{12,8},{14,10},{16,20},{18,... | collective-permute-start | bytes 1769480 | tf_op jit(solution)/shard_map/ppermute | solution.py:896
  110.0 29.4 %collective-permute-start.2 = (bf16[4,48,1536]{2,1,0:T(8,128)(2,1)}, bf16[4,48,1536]{2,1,0:T(8,128)(2,1)}, u32[]{:S(2)}, u32[]{:S(2)}) collective-permute-start(bf16[4,48,1536]{2,1,0:T(8,128)(2,1)} %get-tuple-element.79), channel_id=1, source_target_pairs={{0,4},{2,6},{4,0},{6,2},{8,12},{10,14},{12,8},{14,10},{16,20},{18,... | collective-permute-start | bytes 1769480 | tf_op jit(solution)/shard_map/ppermute | solution.py:896
  111.3 28.3 %collective-permute-start = (bf16[784,768]{1,0:T(8,128)(2,1)}, bf16[784,768]{1,0:T(8,128)(2,1)}, u32[]{:S(2)}, u32[]{:S(2)}) collective-permute-start(bf16[784,768]{1,0:T(8,128)(2,1)} %get-tuple-element.74), channel_id=1, source_target_pairs={{0,1},{1,0},{2,3},{3,2},{4,5},{5,4},{6,7},{7,6},{8,9},{9,8},{10,11... | collective-permute-start | bytes 3612680 | tf_op jit(solution)/shard_map/ppermute | solution.py:899
  139.4 0.8 copy-start
